TPU v7x, 32 devices: a whole 2x2x4 slice. The times are simulated.
32 devices in a mesh: scen: 2 (over x), tm: 16 (over z, y, core).
Axes of the slice: x: 2, y: 2, z: 4, core: 2. Of those that a mesh axis runs over, the one named last changes fastest.
Arguments:
- states: bfloat16 [64, 384], P(('scen', 'tm')), parts along dimension 0, may hold values from -6 to 6
- gradient: float32 [64, 384], P(('scen', 'tm')), parts along dimension 0, may hold values from -0.1 to 0.1
- active_mask: int32 [64, 384], P(('scen', 'tm')), parts along dimension 0, may hold values 0 or 1
- zone_weight: float32 [64, 16], P(('scen', 'tm')), parts along dimension 0, may hold values from 0.001 to 0.004
- zone_map: int32 [768], P('scen'), parts along dimension 0, may hold values from 0 to 15
- w_in: bfloat16 [384, 2048], P('tm'), may hold values from -0.3125 to 0.3125
- w_out: bfloat16 [2048, 384], replicated, may hold values from -0.0625 to 0.0625
- bias: float32 [2048], replicated, may hold values from -3 to 3
Outputs:
- step: float32 [64, 384], P(('scen', 'tm')), parts along dimension 0
There are 2 independent parts, one for each index of `scen`. A program takes and returns all parts, laid end to end along the dimension named above; an argument that names none is the same for every part. Nothing has to cross between parts.
Inputs may be any that keep to these rules, and one draw needn't show every extreme that they name: `zone_map`: each entry names one of the 16 zones.
All inputs are finite; a program needn't handle non-finite values. No bound on the sum of `active_mask` on one device may be relied on, other than what follows from the above.
Results may differ from a plain program's by a relative error of at most 0.0035.
Values may be sent and summed in bfloat16 or wider, within the bound.
A program may use at most 128 MiB of HBM per device.

v0:
```python
import jax
import jax.numpy as jnp
from jax import lax
from jax.sharding import PartitionSpec as P

RHO = 1.0


def from_partner(array, axis, bit):
    return lax.ppermute(array, axis, [(i, i ^ 1 << bit) for i in range(lax.axis_size(axis))])


def matmul(left, right):
    return jnp.dot(left, right, precision=lax.Precision.HIGHEST)


def inverse_factor(matrix):
    width = matrix.shape[0]
    factor = jnp.linalg.cholesky(matrix)
    return jax.scipy.linalg.solve_triangular(factor, jnp.eye(width, dtype=matrix.dtype), lower=True)


def merge_pair(lower, upper, guard):
    middle = lower[2] + upper[0] + guard
    middle_rhs = lower[4] + upper[3]
    inverse = inverse_factor(middle)
    left_solved = matmul(inverse, lower[1].T)
    right_solved = matmul(inverse, upper[1])
    rhs_solved = matmul(inverse, middle_rhs)
    first_first = lower[0] - matmul(left_solved.T, left_solved)
    first_last = -matmul(left_solved.T, right_solved)
    last_last = upper[2] - matmul(right_solved.T, right_solved)
    first_rhs = lower[3] - matmul(left_solved.T, rhs_solved)
    last_rhs = upper[4] - matmul(right_solved.T, rhs_solved)
    return (
        (first_first, first_last, last_last, first_rhs, last_rhs),
        (inverse, left_solved, right_solved, rhs_solved),
    )


def back_solve(store, outer_first, outer_last):
    inverse, left_solved, right_solved, rhs_solved = store
    value = rhs_solved - matmul(left_solved, outer_first) - matmul(right_solved, outer_last)
    return matmul(inverse.T, value)


def element_blocks(jacobian, weight_row, grad_row):
    width = jacobian.shape[0]
    first_first = jnp.diag(weight_row) + RHO * matmul(jacobian, jacobian.T)
    first_last = -RHO * jacobian
    last_last = RHO * jnp.eye(width, dtype=jnp.float32)
    return (first_first, first_last, last_last, grad_row, jnp.zeros_like(grad_row))


def solve_ends(chain):
    width = chain[0].shape[0]
    top = jnp.concatenate([chain[0], chain[1]], axis=1)
    bottom = jnp.concatenate([chain[1].T, chain[2]], axis=1)
    system = jnp.concatenate([top, bottom], axis=0)
    inverse = inverse_factor(system)
    rhs = jnp.concatenate([chain[3], chain[4]])
    ends = matmul(inverse.T, matmul(inverse, rhs))
    return (ends[:width], ends[width:])


def per_device(states, gradient, active_mask, zone_weight, zone_map, w_in, w_out, bias):
    section_rows = states.shape[0]
    width = states.shape[1]
    devices = lax.axis_size("tm")
    place = lax.axis_index("tm")
    whole_rows = lax.all_gather(w_in, "tm", axis=0, tiled=True)
    hidden_in = jnp.dot(states, whole_rows, preferred_element_type=jnp.float32) + bias
    slopes = (1.0 - jnp.tanh(hidden_in) ** 2).astype(jnp.bfloat16)
    weighted = slopes[:, None, :] * whole_rows[None, :, :]
    flat = weighted.reshape(section_rows * width, whole_rows.shape[1])
    product = jnp.dot(flat, w_out, preferred_element_type=jnp.float32).reshape(
        section_rows, width, width
    )
    jacobians = product + jnp.eye(width, dtype=jnp.float32)[None, :, :]
    zone_count = zone_weight.shape[1]
    zone_table = (
        zone_map[None, :] == lax.broadcasted_iota(jnp.int32, (zone_count, width), 0)
    ).astype(jnp.float32)
    weights = matmul(zone_weight, zone_table) * (1.0 + 4.0 * active_mask.astype(jnp.float32))
    own = element_blocks(jacobians[0], weights[0], gradient[0])
    item = element_blocks(jacobians[1], weights[1], gradient[1])
    own, store = merge_pair(own, item, 0.0)
    local_stores = [store]
    level_count = devices.bit_length() - 1
    level_stores = []
    for level in range(level_count):
        partner = from_partner((own[0], own[1], own[2], own[3], own[4]), "tm", level)
        upper_flag = jnp.bitwise_and(jnp.right_shift(place, level), 1) == 1
        lower = jax.tree.map(
            lambda first_part, second_part: jnp.where(upper_flag, first_part, second_part),
            tuple(partner),
            own,
        )
        upper = jax.tree.map(
            lambda first_part, second_part: jnp.where(upper_flag, first_part, second_part),
            own,
            tuple(partner),
        )
        own, store = merge_pair(lower, upper, 0.0)
        level_stores.append((store, upper_flag))
    start_state, end_state = solve_ends(own)
    for store, upper_flag in reversed(level_stores):
        middle = back_solve(store, start_state, end_state)
        start_state = jnp.where(upper_flag, middle, start_state)
        end_state = jnp.where(upper_flag, end_state, middle)
    later_state = end_state
    rows = []
    for store in reversed(local_stores):
        middle = back_solve(store, start_state, later_state)
        rows.insert(0, middle)
        later_state = middle
    return jnp.stack([start_state] + rows, axis=0)


def solution(mesh):
    return jax.shard_map(
        per_device,
        mesh=mesh,
        in_specs=(
            P(("scen", "tm"), None),
            P(("scen", "tm"), None),
            P(("scen", "tm"), None),
            P(("scen", "tm"), None),
            P("scen"),
            P("tm", None),
            P(),
            P(),
        ),
        out_specs=P(("scen", "tm"), None),
        check_vma=False,
    )
```

profile of v0, /device:TPU:0, one launch (start us, length us, event | category | flops | bytes accessed | tf_op | source)
XLA Modules:
  0.0 1072.5 jit_solution(17950450528249653888)
XLA Ops:
  12.8 39.2 %all-gather.2.cloned.1.call-done = bf16[384,2048]{1,0:T(8,128)(2,1)} async-done(((bf16[24,2048]{1,0:T(8,128)(2,1)}), bf16[384,2048]{1,0:T(8,128)(2,1)}) %all-gather.2.cloned.1.call-update) | async-done | bytes 1572880 | tf_op jit(solution)/shard_map/all_gather | solution.py:71
  59.6 11.7 %cholesky.719 = f32[128,128]{1,0:T(8,128)S(1)} custom-call(f32[128,128]{1,0:T(8,128)S(1)} %cholesky.925), custom_call_target="Cholesky" | custom-call | tf_op jit(solution)/shard_map/jit(cholesky)/cholesky | solution.py:19
  81.8 11.9 %cholesky.731 = f32[128,128]{1,0:T(8,128)S(1)} custom-call(f32[128,128]{1,0:T(8,128)S(1)} %cholesky.929), custom_call_target="Cholesky" | custom-call | tf_op jit(solution)/shard_map/jit(cholesky)/cholesky | solution.py:19
  125.5 29.7 %custom-call.82 = f32[3,128,128]{1,2,0:T(8,128)S(1)} custom-call(f32[3,128,128]{2,1,0:T(8,128)S(1)} %get-tuple-element.49), custom_call_target="InvertDiagBlocksLowerTriangular" | custom-call | tf_op jit(solution)/shard_map/jit(_solve_triangular)/triangular_solve | solution.py:20
  247.4 29.7 %custom-call.85 = f32[3,128,128]{1,2,0:T(8,128)S(1)} custom-call(f32[3,128,128]{2,1,0:T(8,128)S(1)} %get-tuple-element.50), custom_call_target="InvertDiagBlocksLowerTriangular" | custom-call | tf_op jit(solution)/shard_map/jit(_solve_triangular)/triangular_solve | solution.py:20
  298.8 16.4 %collective-permute-done.8 = f32[384]{0:T(512)S(1)} collective-permute-done((f32[384]{0:T(512)S(1)}, f32[384]{0:T(512)S(1)}, u32[]{:S(2)}, u32[]{:S(2)}) %collective-permute-start.8) | collective-permute-done | bytes 1568 | tf_op jit(solution)/shard_map/ppermute | solution.py:10
  320.8 12.2 %cholesky.803 = f32[128,128]{1,0:T(8,128)S(1)} custom-call(f32[128,128]{1,0:T(8,128)S(1)} %cholesky.941), custom_call_target="Cholesky" | custom-call | tf_op jit(solution)/shard_map/jit(cholesky)/cholesky | solution.py:19
  368.1 11.9 %cholesky.830 = f32[128,128]{1,0:T(8,128)S(1)} custom-call(f32[128,128]{1,0:T(8,128)S(1)} %convolution_subtract_fusion.23), custom_call_target="Cholesky" | custom-call | tf_op jit(solution)/shard_map/jit(cholesky)/cholesky | solution.py:19
  393.2 29.5 %custom-call.88 = f32[3,128,128]{1,2,0:T(8,128)S(1)} custom-call(f32[3,128,128]{2,1,0:T(8,128)S(1)} %get-tuple-element.51), custom_call_target="InvertDiagBlocksLowerTriangular" | custom-call | tf_op jit(solution)/shard_map/jit(_solve_triangular)/triangular_solve | solution.py:20
  444.4 16.8 %collective-permute-done.13 = f32[384]{0:T(512)S(1)} collective-permute-done((f32[384]{0:T(512)S(1)}, f32[384]{0:T(512)S(1)}, u32[]{:S(2)}, u32[]{:S(2)}) %collective-permute-start.13) | collective-permute-done | bytes 1568 | tf_op jit(solution)/shard_map/ppermute | solution.py:10
  466.7 12.1 %cholesky.845 = f32[128,128]{1,0:T(8,128)S(1)} custom-call(f32[128,128]{1,0:T(8,128)S(1)} %cholesky.949), custom_call_target="Cholesky" | custom-call | tf_op jit(solution)/shard_map/jit(cholesky)/cholesky | solution.py:19
  513.9 11.9 %cholesky.872 = f32[128,128]{1,0:T(8,128)S(1)} custom-call(f32[128,128]{1,0:T(8,128)S(1)} %convolution_subtract_fusion.22), custom_call_target="Cholesky" | custom-call | tf_op jit(solution)/shard_map/jit(cholesky)/cholesky | solution.py:19
  539.0 29.5 %custom-call.91 = f32[3,128,128]{1,2,0:T(8,128)S(1)} custom-call(f32[3,128,128]{2,1,0:T(8,128)S(1)} %get-tuple-element.52), custom_call_target="InvertDiagBlocksLowerTriangular" | custom-call | tf_op jit(solution)/shard_map/jit(_solve_triangular)/triangular_solve | solution.py:20
  591.8 54.1 %collective-permute-done.18 = f32[384]{0:T(512)S(1)} collective-permute-done((f32[384]{0:T(512)S(1)}, f32[384]{0:T(512)S(1)}, u32[]{:S(2)}, u32[]{:S(2)}) %collective-permute-start.18) | collective-permute-done | bytes 1568 | tf_op jit(solution)/shard_map/ppermute | solution.py:10
  650.8 12.1 %cholesky.887 = f32[128,128]{1,0:T(8,128)S(1)} custom-call(f32[128,128]{1,0:T(8,128)S(1)} %cholesky.957), custom_call_target="Cholesky" | custom-call | tf_op jit(solution)/shard_map/jit(cholesky)/cholesky | solution.py:19
  698.1 11.9 %cholesky.914 = f32[128,128]{1,0:T(8,128)S(1)} custom-call(f32[128,128]{1,0:T(8,128)S(1)} %convolution_subtract_fusion.21), custom_call_target="Cholesky" | custom-call | tf_op jit(solution)/shard_map/jit(cholesky)/cholesky | solution.py:19
  723.3 29.5 %custom-call.94 = f32[3,128,128]{1,2,0:T(8,128)S(1)} custom-call(f32[3,128,128]{2,1,0:T(8,128)S(1)} %get-tuple-element.53), custom_call_target="InvertDiagBlocksLowerTriangular" | custom-call | tf_op jit(solution)/shard_map/jit(_solve_triangular)/triangular_solve | solution.py:20
  809.0 13.2 %cholesky.281 = f32[128,128]{1,0:T(8,128)} custom-call(f32[128,128]{1,0:T(8,128)} %cholesky.969), custom_call_target="Cholesky" | custom-call | tf_op jit(solution)/shard_map/jit(cholesky)/cholesky | solution.py:19
  839.9 13.2 %cholesky.437 = f32[128,128]{1,0:T(8,128)} custom-call(f32[128,128]{1,0:T(8,128)} %cholesky.974), custom_call_target="Cholesky" | custom-call | tf_op jit(solution)/shard_map/jit(cholesky)/cholesky | solution.py:19
  870.4 13.5 %cholesky.456 = f32[128,128]{1,0:T(8,128)} custom-call(f32[128,128]{1,0:T(8,128)} %cholesky.979), custom_call_target="Cholesky" | custom-call | tf_op jit(solution)/shard_map/jit(cholesky)/cholesky | solution.py:19
  901.2 13.2 %cholesky.471 = f32[128,128]{1,0:T(8,128)} custom-call(f32[128,128]{1,0:T(8,128)} %cholesky.984), custom_call_target="Cholesky" | custom-call | tf_op jit(solution)/shard_map/jit(cholesky)/cholesky | solution.py:19
  930.7 13.3 %cholesky.485 = f32[128,128]{1,0:T(8,128)} custom-call(f32[128,128]{1,0:T(8,128)} %slice_subtract_fusion.4), custom_call_target="Cholesky" | custom-call | tf_op jit(solution)/shard_map/jit(cholesky)/cholesky | solution.py:19
  957.1 20.8 %while.11 = (s32[]{:T(128)}, f32[768,768]{1,0:T(8,128)}, s32[6,2]{0,1:T(2,128)S(1)}, f32[6,128,128]{2,1,0:T(8,128)}, s32[]{:T(128)}) while((s32[]{:T(128)}, f32[768,768]{1,0:T(8,128)}, s32[6,2]{0,1:T(2,128)S(1)}, f32[6,128,128]{2,1,0:T(8,128)}, s32[]{:T(128)}) %tuple.166), condition=%wide.while_cond.1, body=%wide.while_body.1.sunk | while | flops 2 | bytes 132205 | solution.py:20
  977.9 60.4 %custom-call.55 = f32[6,128,128]{1,2,0:T(8,128)} custom-call(f32[6,128,128]{2,1,0:T(8,128)} %get-tuple-element.24), custom_call_target="InvertDiagBlocksLowerTriangular" | custom-call | tf_op jit(solution)/shard_map/jit(_solve_triangular)/triangular_solve | solution.py:20
  (665 shorter events, 586.0 us)
Async XLA Ops:
  6.5 45.4 %all-gather.2.cloned.1.call-start = ((), (), s32[]{:S(2)}) async-start(), calls=%async_computation | async-start | bytes 1671168 | tf_op jit(solution)/shard_map/all_gather | solution.py:71
  166.5 3.5 collective-permute-start.1
  166.8 3.2 collective-permute-start
  167.1 2.3 collective-permute-start.3
  167.3 2.1 collective-permute-start.2
  169.0 115.1 %collective-permute-start.4 = (f32[384,384]{0,1:T(8,128)S(1)}, f32[384,384]{0,1:T(8,128)}, u32[]{:S(2)}, u32[]{:S(2)}) collective-permute-start(f32[384,384]{0,1:T(8,128)S(1)} %convolution_negate_fusion.4), channel_id=1, source_target_pairs={{0,1},{1,0},{2,3},{3,2},{4,5},{5,4},{6,7},{7,6},{8,9},{9,8},{10,11... | collective-permute-start | bytes 1769480 | tf_op jit(solution)/shard_map/ppermute | solution.py:10
  286.7 29.2 %collective-permute-start.6 = (f32[384,384]{0,1:T(8,128)S(1)}, f32[384,384]{0,1:T(8,128)S(1)}, u32[]{:S(2)}, u32[]{:S(2)}) collective-permute-start(f32[384,384]{0,1:T(8,128)S(1)} %select_subtract_fusion.6), channel_id=1, source_target_pairs={{0,2},{1,3},{2,0},{3,1},{4,6},{5,7},{6,4},{7,5},{8,10},{9,11},{10,... | collective-permute-start | bytes 1769480 | tf_op jit(solution)/shard_map/ppermute | solution.py:10
  293.3 22.7 %collective-permute-start.5 = (f32[384,384]{0,1:T(8,128)S(1)}, f32[384,384]{0,1:T(8,128)S(1)}, u32[]{:S(2)}, u32[]{:S(2)}) collective-permute-start(f32[384,384]{0,1:T(8,128)S(1)} %select_subtract_fusion.7), channel_id=1, source_target_pairs={{0,2},{1,3},{2,0},{3,1},{4,6},{5,7},{6,4},{7,5},{8,10},{9,11},{10,... | collective-permute-start | bytes 1769480 | tf_op jit(solution)/shard_map/ppermute | solution.py:10
  294.8 20.5 %collective-permute-start.8 = (f32[384]{0:T(512)S(1)}, f32[384]{0:T(512)S(1)}, u32[]{:S(2)}, u32[]{:S(2)}) collective-permute-start(f32[384]{0:T(512)S(1)} %select_subtract_fusion.14), channel_id=1, source_target_pairs={{0,2},{1,3},{2,0},{3,1},{4,6},{5,7},{6,4},{7,5},{8,10},{9,11},{10,... | collective-permute-start | bytes 4616 | tf_op jit(solution)/shard_map/ppermute | solution.py:10
  295.4 19.9 %collective-permute-start.7 = (f32[384]{0:T(512)S(1)}, f32[384]{0:T(512)S(1)}, u32[]{:S(2)}, u32[]{:S(2)}) collective-permute-start(f32[384]{0:T(512)S(1)} %select_subtract_fusion.15), channel_id=1, source_target_pairs={{0,2},{1,3},{2,0},{3,1},{4,6},{5,7},{6,4},{7,5},{8,10},{9,11},{10,... | collective-permute-start | bytes 4616 | tf_op jit(solution)/shard_map/ppermute | solution.py:10
  298.2 131.4 %collective-permute-start.9 = (f32[384,384]{0,1:T(8,128)S(1)}, f32[384,384]{0,1:T(8,128)}, u32[]{:S(2)}, u32[]{:S(2)}) collective-permute-start(f32[384,384]{0,1:T(8,128)S(1)} %convolution_negate_fusion.3), channel_id=1, source_target_pairs={{0,2},{1,3},{2,0},{3,1},{4,6},{5,7},{6,4},{7,5},{8,10},{9,11},{10,... | collective-permute-start | bytes 1769480 | tf_op jit(solution)/shard_map/ppermute | solution.py:10
  432.2 29.6 %collective-permute-start.11 = (f32[384,384]{0,1:T(8,128)S(1)}, f32[384,384]{0,1:T(8,128)S(1)}, u32[]{:S(2)}, u32[]{:S(2)}) collective-permute-start(f32[384,384]{0,1:T(8,128)S(1)} %select_subtract_fusion.4), channel_id=1, source_target_pairs={{0,4},{1,5},{2,6},{3,7},{4,0},{5,1},{6,2},{7,3},{8,12},{9,13},{10,... | collective-permute-start | bytes 1769480 | tf_op jit(solution)/shard_map/ppermute | solution.py:10
  438.7 23.1 %collective-permute-start.10 = (f32[384,384]{0,1:T(8,128)S(1)}, f32[384,384]{0,1:T(8,128)S(1)}, u32[]{:S(2)}, u32[]{:S(2)}) collective-permute-start(f32[384,384]{0,1:T(8,128)S(1)} %select_subtract_fusion.5), channel_id=1, source_target_pairs={{0,4},{1,5},{2,6},{3,7},{4,0},{5,1},{6,2},{7,3},{8,12},{9,13},{10,... | collective-permute-start | bytes 1769480 | tf_op jit(solution)/shard_map/ppermute | solution.py:10
  440.3 20.8 %collective-permute-start.13 = (f32[384]{0:T(512)S(1)}, f32[384]{0:T(512)S(1)}, u32[]{:S(2)}, u32[]{:S(2)}) collective-permute-start(f32[384]{0:T(512)S(1)} %select_subtract_fusion.12), channel_id=1, source_target_pairs={{0,4},{1,5},{2,6},{3,7},{4,0},{5,1},{6,2},{7,3},{8,12},{9,13},{10,... | collective-permute-start | bytes 4616 | tf_op jit(solution)/shard_map/ppermute | solution.py:10
  440.9 20.3 %collective-permute-start.12 = (f32[384]{0:T(512)S(1)}, f32[384]{0:T(512)S(1)}, u32[]{:S(2)}, u32[]{:S(2)}) collective-permute-start(f32[384]{0:T(512)S(1)} %select_subtract_fusion.13), channel_id=1, source_target_pairs={{0,4},{1,5},{2,6},{3,7},{4,0},{5,1},{6,2},{7,3},{8,12},{9,13},{10,... | collective-permute-start | bytes 4616 | tf_op jit(solution)/shard_map/ppermute | solution.py:10
  443.9 131.5 %collective-permute-start.14 = (f32[384,384]{0,1:T(8,128)S(1)}, f32[384,384]{0,1:T(8,128)}, u32[]{:S(2)}, u32[]{:S(2)}) collective-permute-start(f32[384,384]{0,1:T(8,128)S(1)} %convolution_negate_fusion.2), channel_id=1, source_target_pairs={{0,4},{1,5},{2,6},{3,7},{4,0},{5,1},{6,2},{7,3},{8,12},{9,13},{10,... | collective-permute-start | bytes 1769480 | tf_op jit(solution)/shard_map/ppermute | solution.py:10
  578.1 68.0 %copy-start.24 = (f32[384,384]{0,1:T(8,128)}, f32[384,384]{0,1:T(8,128)S(1)}, u32[]{:S(2)}) copy-start(f32[384,384]{0,1:T(8,128)S(1)} %select_subtract_fusion.2) | copy-start | bytes 1769476
  578.1 67.9 %collective-permute-start.16 = (f32[384,384]{0,1:T(8,128)S(1)}, f32[384,384]{0,1:T(8,128)S(1)}, u32[]{:S(2)}, u32[]{:S(2)}) collective-permute-start(f32[384,384]{0,1:T(8,128)S(1)} %select_subtract_fusion.2), channel_id=1, source_target_pairs={{0,8},{1,9},{2,10},{3,11},{4,12},{5,13},{6,14},{7,15},{8,0},{9,1},... | collective-permute-start | bytes 1769480 | tf_op jit(solution)/shard_map/ppermute | solution.py:10
  584.4 61.6 %collective-permute-start.15 = (f32[384,384]{0,1:T(8,128)S(1)}, f32[384,384]{0,1:T(8,128)S(1)}, u32[]{:S(2)}, u32[]{:S(2)}) collective-permute-start(f32[384,384]{0,1:T(8,128)S(1)} %select_subtract_fusion.3), channel_id=1, source_target_pairs={{0,8},{1,9},{2,10},{3,11},{4,12},{5,13},{6,14},{7,15},{8,0},{9,1},... | collective-permute-start | bytes 1769480 | tf_op jit(solution)/shard_map/ppermute | solution.py:10
  587.0 58.9 %collective-permute-start.18 = (f32[384]{0:T(512)S(1)}, f32[384]{0:T(512)S(1)}, u32[]{:S(2)}, u32[]{:S(2)}) collective-permute-start(f32[384]{0:T(512)S(1)} %select_subtract_fusion.10), channel_id=1, source_target_pairs={{0,8},{1,9},{2,10},{3,11},{4,12},{5,13},{6,14},{7,15},{8,0},{9,1},... | collective-permute-start | bytes 4616 | tf_op jit(solution)/shard_map/ppermute | solution.py:10
  587.5 58.5 %collective-permute-start.17 = (f32[384]{0:T(512)S(1)}, f32[384]{0:T(512)S(1)}, u32[]{:S(2)}, u32[]{:S(2)}) collective-permute-start(f32[384]{0:T(512)S(1)} %select_subtract_fusion.11), channel_id=1, source_target_pairs={{0,8},{1,9},{2,10},{3,11},{4,12},{5,13},{6,14},{7,15},{8,0},{9,1},... | collective-permute-start | bytes 4616 | tf_op jit(solution)/shard_map/ppermute | solution.py:10
  591.4 167.1 %copy-start.21 = (f32[384,384]{0,1:T(8,128)}, f32[384,384]{0,1:T(8,128)S(1)}, u32[]{:S(2)}) copy-start(f32[384,384]{0,1:T(8,128)S(1)} %convolution_negate_fusion.1) | copy-start | bytes 1769476
  591.4 167.1 %collective-permute-start.19 = (f32[384,384]{0,1:T(8,128)S(1)}, f32[384,384]{0,1:T(8,128)}, u32[]{:S(2)}, u32[]{:S(2)}) collective-permute-start(f32[384,384]{0,1:T(8,128)S(1)} %convolution_negate_fusion.1), channel_id=1, source_target_pairs={{0,8},{1,9},{2,10},{3,11},{4,12},{5,13},{6,14},{7,15},{8,0},{9,1},... | collective-permute-start | bytes 1769480 | tf_op jit(solution)/shard_map/ppermute | solution.py:10
  957.1 84.5 %copy-start.18 = (f32[768,768]{1,0:T(8,128)S(1)}, f32[768,768]{1,0:T(8,128)}, u32[]{:S(2)}) copy-start(f32[768,768]{1,0:T(8,128)} %fusion.48) | copy-start | bytes 7077892
  (126 other events, 886.8 us)
Sparse Core Ops, SparseCore 0:
  9.6 42.3 all-gather.1
where the time goes:
time: 1080 us; the launch traced here: 1070 us
  other arithmetic  664 us (61%)
  matrix products  139 us (13%)
  waiting for transfers between devices  128 us (12%)
  local copies, waits for them, and re-layouts  93.8 us (9%)
  between operations  30 us (3%)
  starting transfers between devices  17.5 us (2%)
    another operation x77, other arithmetic, inverse_factor(): factor = jnp.linalg.cholesky(matrix)  437 us
    another operation x14, other arithmetic, inverse_factor(): jax.scipy.linalg.solve_triangular(factor, jnp.eye(width, dtype=matrix.dty...  214 us
    ppermute x20, waiting for transfers between devices, from_partner(): lax.ppermute(array, axis, [(i, i ^ 1 << bit) for i in range(lax.axis_size...  87.7 us
    dot_general x60, matrix products, matmul(): return jnp.dot(left, right, precision=lax.Precision.HIGHEST)  66.5 us
    another operation x52, local copies, waits for them, and re-layouts, inverse_factor(): jax.scipy.linalg.solve_triangular(factor, jnp.eye(width, dtype=matrix.dty...  40.2 us
    all_gather x1, waiting for transfers between devices, per_device(): whole_rows = lax.all_gather(w_in, 'tm', axis=0, tiled=True)  39.2 us
    another operation x36, matrix products, inverse_factor(): jax.scipy.linalg.solve_triangular(factor, jnp.eye(width, dtype=matrix.dty...  37.9 us
    another operation x30, matrix products, inverse_factor(): factor = jnp.linalg.cholesky(matrix)  29.8 us
  transfers between devices with their start and end apart: 21, of which 5 were waited for; matrix products, arithmetic and copies ran while one was open for 43% of the time, Pallas kernels for 0%

commit v1 on v0

v1 whole, which is shorter than its diff:
```python
import jax
import jax.numpy as jnp
from jax import lax
from jax.experimental import pallas as pl
from jax.experimental.pallas import tpu as pltpu
from jax.sharding import PartitionSpec as P


def from_partner(array, axis, bit):
    return lax.ppermute(array, axis, [(i, i ^ 1 << bit) for i in range(lax.axis_size(axis))])


def matmul(left, right):
    return jnp.dot(left, right, precision=lax.Precision.HIGHEST)


def dot_exact(left, right, dims=((1,), (0,))):
    return lax.dot_general(
        left, right, (dims, ((), ())), precision=lax.Precision.HIGHEST, preferred_element_type=jnp.float32
    )


def dot_fast(left, right):
    return jnp.dot(
        left.astype(jnp.bfloat16), right.astype(jnp.bfloat16), preferred_element_type=jnp.float32
    )


def invert_in_place(m_ref, x_ref, e_ref):
    width = m_ref.shape[0]
    row_ids = lax.broadcasted_iota(jnp.int32, (width, width), 0)
    col_ids = lax.broadcasted_iota(jnp.int32, (width, width), 1)
    diagonal = row_ids == col_ids
    matrix = m_ref[...]
    square = dot_fast(matrix, matrix)
    trace = jnp.sum(jnp.where(diagonal, matrix, 0.0))
    frobenius = jnp.sum(matrix * matrix)
    bound = jnp.max(jnp.sum(jnp.abs(square), axis=1))
    scale = jnp.minimum(trace / frobenius, 1.9 * lax.rsqrt(bound))
    x_ref[...] = jnp.where(diagonal, 2.0 * scale, 0.0) - (scale * scale) * matrix
    first = jnp.where(diagonal, 1.0, 0.0) - (2.0 * scale) * matrix + (scale * scale) * square
    e_ref[...] = first

    def coarse_step(carry):
        count, _ = carry
        x_ref[...] = x_ref[...] + dot_fast(x_ref[...], e_ref[...])
        residual = jnp.where(diagonal, 1.0, 0.0) - dot_fast(m_ref[...], x_ref[...])
        e_ref[...] = residual
        return count + 1, jnp.sum(residual * residual)

    lax.while_loop(lambda c: (c[0] < 10) & (c[1] > 0.25), coarse_step, (0, jnp.sum(first * first)))

    def fine_step(carry):
        count, _ = carry
        residual = jnp.where(diagonal, 1.0, 0.0) - dot_exact(m_ref[...], x_ref[...])
        x_ref[...] = x_ref[...] + dot_exact(x_ref[...], residual)
        return count + 1, jnp.sum(residual * residual)

    _, last = lax.while_loop(
        lambda c: (c[0] < 12) & jnp.logical_not(c[1] <= 1e-7), fine_step, (0, jnp.float32(1.0))
    )

    @pl.when(jnp.logical_not(last <= 1e-7))
    def _():
        x_ref[...] = m_ref[...]

        def pivot_step(k, carry):
            current = x_ref[...]
            row = x_ref[pl.ds(k, 1), :]
            column = jnp.sum(jnp.where(col_ids == k, current, 0.0), axis=1, keepdims=True)
            pivot = jnp.sum(jnp.where(col_ids[:1] == k, row, 0.0), axis=1, keepdims=True)
            scaled = row / pivot
            updated = jnp.where(col_ids == k, -column / pivot, current - column * scaled)
            own_row = jnp.where(col_ids == k, 1.0 / pivot, scaled)
            x_ref[...] = jnp.where(row_ids == k, own_row, updated)
            return carry

        lax.fori_loop(0, width, pivot_step, 0)


def eliminate_kernel(
    m_ref, mr_ref, l_ref, r_ref, ff_ref, ll_ref, fr_ref, lr_ref,
    off_ref, ofl_ref, oll_ref, ofr_ref, olr_ref, gl_ref, gr_ref, gs_ref, x_ref, e_ref
):
    width = m_ref.shape[0]
    invert_in_place(m_ref, x_ref, e_ref)
    inverse = x_ref[...]
    left = l_ref[...]
    right = r_ref[...]
    gl_ref[...] = dot_exact(left, inverse)
    gr_ref[...] = dot_exact(inverse, right)
    solved = dot_exact(jnp.broadcast_to(mr_ref[...], (8, width)), inverse)
    gs_ref[...] = solved[:1]
    off_ref[...] = ff_ref[...] - dot_exact(gl_ref[...], left, ((1,), (1,)))
    ofl_ref[...] = -dot_exact(gl_ref[...], right)
    oll_ref[...] = ll_ref[...] - dot_exact(jnp.transpose(right), gr_ref[...])
    ofr_ref[...] = fr_ref[...] - dot_exact(solved, left, ((1,), (1,)))[:1]
    olr_ref[...] = lr_ref[...] - dot_exact(solved, right)[:1]


def eliminate(*parts):
    width = parts[0].shape[0]
    full = jax.ShapeDtypeStruct((width, width), jnp.float32)
    row = jax.ShapeDtypeStruct((1, width), jnp.float32)
    result = pl.pallas_call(
        eliminate_kernel,
        out_shape=(full, full, full, row, row, full, full, row),
        scratch_shapes=[pltpu.VMEM((width, width), jnp.float32)] * 2,
        compiler_params=pltpu.CompilerParams(vmem_limit_bytes=48 << 20),
        name="eliminate",
    )(*[part if part.ndim == 2 else part[None] for part in parts])
    return result[:5], result[5:]


def root_kernel(m_ref, mr_ref, o_ref, x_ref, e_ref):
    invert_in_place(m_ref, x_ref, e_ref)
    o_ref[...] = dot_exact(jnp.broadcast_to(mr_ref[...], (8, m_ref.shape[0])), x_ref[...])[:1]


def root_solve(matrix, rhs):
    width = matrix.shape[0]
    return pl.pallas_call(
        root_kernel,
        out_shape=jax.ShapeDtypeStruct((1, width), jnp.float32),
        scratch_shapes=[pltpu.VMEM((width, width), jnp.float32)] * 2,
        compiler_params=pltpu.CompilerParams(vmem_limit_bytes=48 << 20),
        name="root",
    )(matrix, rhs)


def per_device(states, gradient, active_mask, zone_weight, zone_map, w_in, w_out, bias):
    width = states.shape[1]
    devices = lax.axis_size("tm")
    place = lax.axis_index("tm")
    is_first = place == 0
    is_last = place == devices - 1
    zone_count = zone_weight.shape[1]
    zone_table = (
        zone_map[None, :] == lax.broadcasted_iota(jnp.int32, (zone_count, width), 0)
    ).astype(jnp.float32)
    weights = jnp.dot(zone_weight, zone_table, precision=lax.Precision.HIGHEST) * (
        1.0 + 4.0 * active_mask.astype(jnp.float32)
    )
    later = jnp.stack([states[1].astype(jnp.float32), gradient[1], weights[1]])
    before = lax.ppermute(later, "tm", [(i, i + 1) for i in range(devices - 1)])
    whole_rows = lax.all_gather(w_in, "tm", axis=0, tiled=True)
    rows = jnp.stack([before[0].astype(jnp.bfloat16), states[0]])
    hidden_in = jnp.dot(rows, whole_rows, preferred_element_type=jnp.float32) + bias
    slopes = (1.0 - jnp.tanh(hidden_in) ** 2).astype(jnp.bfloat16)
    weighted = slopes[:, None, :] * whole_rows[None, :, :]
    flat = weighted.reshape(2 * width, whole_rows.shape[1])
    product = jnp.dot(flat, w_out, preferred_element_type=jnp.float32).reshape(2, width, width)
    eye = jnp.eye(width, dtype=jnp.float32)
    jac_before = product[0] + eye
    jac_own = product[1] + eye
    last_diag = 1.0 / (1.0 + weights[1])
    column_scale = jnp.where(is_last, weights[1] * last_diag, 1.0)
    tail = jnp.where(is_last, gradient[1] * last_diag, 0.0)
    middle = (
        jnp.diag(weights[0] + jnp.where(is_first, 0.0, 1.0))
        + matmul(jac_own * column_scale[None, :], jac_own.T)
    )
    middle_rhs = gradient[0] + matmul(jac_own, tail)
    left = jnp.where(is_first, 0.0, -jac_before)
    right = jnp.where(is_last, 0.0, -jac_own)
    first_first = jnp.diag(before[2]) + matmul(left, left.T)
    own, local_store = eliminate(
        middle, middle_rhs, left, right, first_first, eye, before[1], jnp.zeros_like(middle_rhs)
    )
    level_count = devices.bit_length() - 1
    level_stores = []
    for level in range(level_count):
        upper_flag = jnp.bitwise_and(jnp.right_shift(place, level), 1) == 1
        if level == level_count - 1:
            block = jnp.where(upper_flag, own[0], own[2])
            vector = jnp.where(upper_flag, own[3], own[4])
            other_block, other_vector = from_partner((block, vector), "tm", level)
            root = root_solve(block + other_block, vector + other_vector)[0]
            break
        partner = from_partner(own, "tm", level)
        lower = [jnp.where(upper_flag, a, b) for a, b in zip(partner, own)]
        upper = [jnp.where(upper_flag, b, a) for a, b in zip(partner, own)]
        own, store = eliminate(
            lower[2] + upper[0], lower[4] + upper[3], lower[1], upper[1],
            lower[0], upper[2], lower[3], upper[4],
        )
        level_stores.append((store, upper_flag))
    top_flag = jnp.right_shift(place, level_count - 1) == 1
    start = jnp.where(top_flag, root, 0.0)
    end = jnp.where(top_flag, 0.0, root)
    for store, upper_flag in reversed(level_stores):
        value = back_solve(store, start, end)
        start = jnp.where(upper_flag, value, start)
        end = jnp.where(upper_flag, end, value)
    value = back_solve(local_store, start, end)
    end = jnp.where(is_last, tail + last_diag * matmul(value, jac_own), end)
    return jnp.stack([value, end], axis=0)


def back_solve(store, outer_first, outer_last):
    left_solved, right_solved, rhs_solved = store
    return rhs_solved[0] - matmul(outer_first, left_solved) - matmul(right_solved, outer_last)


def solution(mesh):
    return jax.shard_map(
        per_device,
        mesh=mesh,
        in_specs=(
            P(("scen", "tm"), None),
            P(("scen", "tm"), None),
            P(("scen", "tm"), None),
            P(("scen", "tm"), None),
            P("scen"),
            P("tm", None),
            P(),
            P(),
        ),
        out_specs=P(("scen", "tm"), None),
        check_vma=False,
    )
```

time: 1080 us -> 307 us (0.28)
  other arithmetic: 664 us -> 10.9 us
  matrix products: 139 us -> 12.5 us
  Pallas kernels: 0 us -> 103 us
  local copies, waits for them, and re-layouts: 93.8 us -> 6.44 us
  between operations: 30 us -> 14.1 us
  waiting for transfers between devices: 128 us -> 141 us
    another operation x92 -> x2, other arithmetic: 651 us -> 0.6 us  [the longest x1 0.59 us: per_device(): return jnp.stack([value, end], axis=0)]
    pallas_call x0 -> x5, Pallas kernels: none -> 103 us  [the longest x4 88.9 us: eliminate(): pl.pallas_call(eliminate_kernel, out_shape=(full, full, full, row, row, f...]
    another operation x66 -> x0, matrix products: 67.7 us -> none  [the longest x36 37.9 us: inverse_factor(): jax.scipy.linalg.solve_triangular(factor, jnp.eye(width, dtype=matrix.dty...]
    another operation x92 -> x2, local copies, waits for them, and re-layouts: 65.6 us -> 0.01 us  [per_device(): return jnp.stack([value, end], axis=0)]
    dot_general x60 -> x12, matrix products: 66.5 us -> 8.03 us  [matmul(): return jnp.dot(left, right, precision=lax.Precision.HIGHEST)]
    ppermute x20 -> x17, waiting for transfers between devices: 87.7 us -> 100 us  [from_partner(): lax.ppermute(array, axis, [(i, i ^ 1 << bit) for i in range(lax.axis_size...]
    unnamed x258 -> x34, local copies, waits for them, and re-layouts: 16.7 us -> 5.6 us
  transfers between devices with their start and end apart: 21 -> 19, of which waited for: 5 -> 6; matrix products, arithmetic and copies ran while one was open for 43% -> 2% of each run, Pallas kernels for 0% -> 0%
where the time goes in v1:
time: 307 us; the launch traced here: 302 us
  waiting for transfers between devices  141 us (46%)
  Pallas kernels  103 us (34%)
  starting transfers between devices  14.5 us (5%)
  between operations  14.1 us (5%)
  matrix products  12.5 us (4%)
  other arithmetic  10.9 us (4%)
  local copies, waits for them, and re-layouts  6.44 us (2%)
    ppermute x17, waiting for transfers between devices, from_partner(): lax.ppermute(array, axis, [(i, i ^ 1 << bit) for i in range(lax.axis_size...  100 us
    pallas_call x4, Pallas kernels, eliminate(): pl.pallas_call(eliminate_kernel, out_shape=(full, full, full, row, row, f...  88.9 us
    all_gather x1, waiting for transfers between devices, per_device(): whole_rows = lax.all_gather(w_in, 'tm', axis=0, tiled=True)  39 us
    pallas_call x1, Pallas kernels, root_solve(): pl.pallas_call(root_kernel, out_shape=jax.ShapeDtypeStruct((1, width), jn...  14.2 us
    ppermute x17, starting transfers between devices, from_partner(): lax.ppermute(array, axis, [(i, i ^ 1 << bit) for i in range(lax.axis_size...  12.1 us
    dot_general x12, matrix products, matmul(): return jnp.dot(left, right, precision=lax.Precision.HIGHEST)  8.03 us
    select_n x9, other arithmetic, per_device(): upper = [jnp.where(upper_flag, b, a) for a, b in zip(partner, own)]  7.71 us
  transfers between devices with their start and end apart: 19, of which 6 were waited for; matrix products, arithmetic and copies ran while one was open for 2% of the time, Pallas kernels for 0%

profile of v1, /device:TPU:0, one launch (start us, length us, event | category | flops | bytes accessed | tf_op | source)
XLA Modules:
  0.0 302.2 jit_solution(11733901446038307243)
XLA Ops:
  9.7 2.4 collective-permute-start
  12.9 39.0 %all-gather.2.cloned.1.call-done = bf16[384,2048]{1,0:T(8,128)(2,1)} async-done(((bf16[24,2048]{1,0:T(8,128)(2,1)}), bf16[384,2048]{1,0:T(8,128)(2,1)}) %all-gather.2.cloned.1.call-update) | async-done | bytes 1572880 | tf_op jit(solution)/shard_map/all_gather | solution.py:146
  52.0 1.9 fusion.3
  54.1 1.8 fusion.33
  57.3 1.3 select_add_fusion.3.ff_ref
  58.6 1.3 convolution_add_fusion.1.m_ref
  60.0 22.6 %eliminate.4 = (f32[384,384]{1,0:T(8,128)S(1)}, f32[384,384]{1,0:T(8,128)}, f32[384,384]{1,0:T(8,128)S(1)}, f32[1,384]{1,0:T(1,128)S(1)}, f32[1,384]{1,0:T(1,128...) custom-call(f32[384,384]{1,0:T(8,128)S(1)} %convolution_add_fusion.1.m_ref, ...), custom_call_target="tpu_custom_call" | custom-call | tf_op jit(solution)/shard_map/eliminate/pallas_call | solution.py:105
  85.3 3.0 collective-permute-done.3
  88.4 1.3 broadcast_select_fusion.10
  89.7 1.3 broadcast_select_fusion.12
  91.0 23.4 %eliminate.5 = (f32[384,384]{1,0:T(8,128)S(1)}, f32[384,384]{1,0:T(8,128)S(1)}, f32[384,384]{1,0:T(8,128)S(1)}, f32[1,384]{1,0:T(1,128)S(1)}, f32[1,384]{1,0:T(1...) custom-call(f32[384,384]{1,0:T(8,128)S(1)} %get-tuple-element.86.m_ref, ...), custom_call_target="tpu_custom_call" | custom-call | tf_op jit(solution)/shard_map/eliminate/pallas_call | solution.py:105
  116.0 2.0 collective-permute-start.6
  118.0 2.0 collective-permute-start.8
  120.1 36.7 %collective-permute-done.8 = f32[1,384]{1,0:T(1,128)S(1)} collective-permute-done((f32[1,384]{1,0:T(1,128)S(1)}, f32[1,384]{1,0:T(1,128)S(1)}, u32[]{:S(2)}, u32[]{:S(2)}) %collective-permute-start.8) | collective-permute-done | bytes 1568 | tf_op jit(solution)/shard_map/ppermute | solution.py:10
  158.0 1.4 broadcast_select_fusion.8
  159.4 20.6 %eliminate.6 = (f32[384,384]{1,0:T(8,128)S(1)}, f32[384,384]{1,0:T(8,128)S(1)}, f32[384,384]{1,0:T(8,128)S(1)}, f32[1,384]{1,0:T(1,128)S(1)}, f32[1,384]{1,0:T(1...) custom-call(f32[384,384]{1,0:T(8,128)S(1)} %get-tuple-element.81.m_ref, ...), custom_call_target="tpu_custom_call" | custom-call | tf_op jit(solution)/shard_map/eliminate/pallas_call | solution.py:105
  181.6 2.0 collective-permute-start.11
  183.7 2.0 collective-permute-start.13
  185.7 35.9 %collective-permute-done.13 = f32[1,384]{1,0:T(1,128)S(1)} collective-permute-done((f32[1,384]{1,0:T(1,128)S(1)}, f32[1,384]{1,0:T(1,128)S(1)}, u32[]{:S(2)}, u32[]{:S(2)}) %collective-permute-start.13) | collective-permute-done | bytes 1568 | tf_op jit(solution)/shard_map/ppermute | solution.py:10
  222.8 1.4 broadcast_select_fusion.4
  224.2 22.3 %eliminate.7 = (f32[384,384]{1,0:T(8,128)S(1)}, f32[384,384]{1,0:T(8,128)}, f32[384,384]{1,0:T(8,128)S(1)}, f32[1,384]{1,0:T(1,128)S(1)}, f32[1,384]{1,0:T(1,128...) custom-call(f32[384,384]{1,0:T(8,128)S(1)} %get-tuple-element.76.m_ref, ...), custom_call_target="tpu_custom_call" | custom-call | tf_op jit(solution)/shard_map/eliminate/pallas_call | solution.py:105
  246.7 2.9 collective-permute-start.17
  249.7 24.4 %collective-permute-done.17 = f32[1,384]{1,0:T(1,128)S(1)} collective-permute-done((f32[1,384]{1,0:T(1,128)S(1)}, f32[1,384]{1,0:T(1,128)S(1)}, u32[]{:S(2)}, u32[]{:S(2)}) %collective-permute-start.17) | collective-permute-done | bytes 1568 | tf_op jit(solution)/shard_map/ppermute | solution.py:10
  275.3 14.2 %root.1 = f32[1,384]{1,0:T(1,128)S(1)} custom-call(f32[384,384]{1,0:T(8,128)S(1)} %add.99.m_ref, f32[1,384]{1,0:T(1,128)S(1)} %add.100.mr_ref), custom_call_target="tpu_custom_call" | custom-call | tf_op jit(solution)/shard_map/root/pallas_call | solution.py:122
  (114 shorter events, 20.9 us)
Async XLA Ops:
  6.5 47.6 %copy-start = (bf16[2048,384]{1,0:T(8,128)(2,1)S(1)}, bf16[2048,384]{1,0:T(8,128)(2,1)}, u32[]{:S(2)}) copy-start(bf16[2048,384]{1,0:T(8,128)(2,1)} %param.14) | copy-start | bytes 4718596
  6.5 45.4 %all-gather.2.cloned.1.call-start = ((), (), s32[]{:S(2)}) async-start(), calls=%async_computation | async-start | bytes 1671168 | tf_op jit(solution)/shard_map/all_gather | solution.py:146
  9.7 3.2 %collective-permute-start = (f32[3,384]{1,0:T(4,128)S(1)}, f32[3,384]{1,0:T(4,128)S(1)}, u32[]{:S(2)}, u32[]{:S(2)}) collective-permute-start(f32[3,384]{1,0:T(4,128)S(1)} %pad_maximum_fusion), channel_id=1, source_target_pairs={{0,1},{1,2},{2,3},{3,4},{4,5},{5,6},{6,7},{7,8},{8,9},{9,10},{10,1... | collective-permute-start | bytes 13832 | tf_op jit(solution)/shard_map/ppermute | solution.py:145
  84.3 4.0 %collective-permute-start.5 = (f32[384,384]{1,0:T(8,128)}, f32[384,384]{1,0:T(8,128)}, u32[]{:S(2)}, u32[]{:S(2)}) collective-permute-start(f32[384,384]{1,0:T(8,128)} %get-tuple-element.41), channel_id=1, source_target_pairs={{0,1},{1,0},{2,3},{3,2},{4,5},{5,4},{6,7},{7,6},{8,9},{9,8},{10,11... | collective-permute-start | bytes 1769480 | tf_op jit(solution)/shard_map/ppermute | solution.py:10
  84.3 5.4 %collective-permute-start.1 = (f32[384,384]{1,0:T(8,128)S(1)}, f32[384,384]{1,0:T(8,128)S(1)}, u32[]{:S(2)}, u32[]{:S(2)}) collective-permute-start(f32[384,384]{1,0:T(8,128)S(1)} %get-tuple-element.37), channel_id=1, source_target_pairs={{0,1},{1,0},{2,3},{3,2},{4,5},{5,4},{6,7},{7,6},{8,9},{9,8},{10,11... | collective-permute-start | bytes 1769480 | tf_op jit(solution)/shard_map/ppermute | solution.py:10
  84.8 4.9 %collective-permute-start.2 = (f32[384,384]{1,0:T(8,128)S(1)}, f32[384,384]{1,0:T(8,128)}, u32[]{:S(2)}, u32[]{:S(2)}) collective-permute-start(f32[384,384]{1,0:T(8,128)S(1)} %get-tuple-element.38), channel_id=1, source_target_pairs={{0,1},{1,0},{2,3},{3,2},{4,5},{5,4},{6,7},{7,6},{8,9},{9,8},{10,11... | collective-permute-start | bytes 1769480 | tf_op jit(solution)/shard_map/ppermute | solution.py:10
  84.8 3.5 %collective-permute-start.3 = (f32[1,384]{1,0:T(1,128)S(1)}, f32[1,384]{1,0:T(1,128)S(1)}, u32[]{:S(2)}, u32[]{:S(2)}) collective-permute-start(f32[1,384]{1,0:T(1,128)S(1)} %get-tuple-element.39), channel_id=1, source_target_pairs={{0,1},{1,0},{2,3},{3,2},{4,5},{5,4},{6,7},{7,6},{8,9},{9,8},{10,11... | collective-permute-start | bytes 4616 | tf_op jit(solution)/shard_map/ppermute | solution.py:10
  85.3 3.0 collective-permute-start.4
  116.0 40.8 %collective-permute-start.10 = (f32[384,384]{1,0:T(8,128)S(1)}, f32[384,384]{1,0:T(8,128)}, u32[]{:S(2)}, u32[]{:S(2)}) collective-permute-start(f32[384,384]{1,0:T(8,128)S(1)} %get-tuple-element.47), channel_id=1, source_target_pairs={{0,2},{1,3},{2,0},{3,1},{4,6},{5,7},{6,4},{7,5},{8,10},{9,11},{10,... | collective-permute-start | bytes 1769480 | tf_op jit(solution)/shard_map/ppermute | solution.py:10
  116.0 42.0 %collective-permute-start.6 = (f32[384,384]{1,0:T(8,128)S(1)}, f32[384,384]{1,0:T(8,128)}, u32[]{:S(2)}, u32[]{:S(2)}) collective-permute-start(f32[384,384]{1,0:T(8,128)S(1)} %get-tuple-element.43), channel_id=1, source_target_pairs={{0,2},{1,3},{2,0},{3,1},{4,6},{5,7},{6,4},{7,5},{8,10},{9,11},{10,... | collective-permute-start | bytes 1769480 | tf_op jit(solution)/shard_map/ppermute | solution.py:10
  118.0 40.0 %collective-permute-start.7 = (f32[384,384]{1,0:T(8,128)S(1)}, f32[384,384]{1,0:T(8,128)}, u32[]{:S(2)}, u32[]{:S(2)}) collective-permute-start(f32[384,384]{1,0:T(8,128)S(1)} %get-tuple-element.44), channel_id=1, source_target_pairs={{0,2},{1,3},{2,0},{3,1},{4,6},{5,7},{6,4},{7,5},{8,10},{9,11},{10,... | collective-permute-start | bytes 1769480 | tf_op jit(solution)/shard_map/ppermute | solution.py:10
  118.0 38.7 %collective-permute-start.8 = (f32[1,384]{1,0:T(1,128)S(1)}, f32[1,384]{1,0:T(1,128)S(1)}, u32[]{:S(2)}, u32[]{:S(2)}) collective-permute-start(f32[1,384]{1,0:T(1,128)S(1)} %get-tuple-element.45), channel_id=1, source_target_pairs={{0,2},{1,3},{2,0},{3,1},{4,6},{5,7},{6,4},{7,5},{8,10},{9,11},{10,... | collective-permute-start | bytes 4616 | tf_op jit(solution)/shard_map/ppermute | solution.py:10
  120.0 36.7 %collective-permute-start.9 = (f32[1,384]{1,0:T(1,128)S(1)}, f32[1,384]{1,0:T(1,128)S(1)}, u32[]{:S(2)}, u32[]{:S(2)}) collective-permute-start(f32[1,384]{1,0:T(1,128)S(1)} %get-tuple-element.46), channel_id=1, source_target_pairs={{0,2},{1,3},{2,0},{3,1},{4,6},{5,7},{6,4},{7,5},{8,10},{9,11},{10,... | collective-permute-start | bytes 4616 | tf_op jit(solution)/shard_map/ppermute | solution.py:10
  181.6 40.0 %collective-permute-start.15 = (f32[384,384]{1,0:T(8,128)S(1)}, f32[384,384]{1,0:T(8,128)}, u32[]{:S(2)}, u32[]{:S(2)}) collective-permute-start(f32[384,384]{1,0:T(8,128)S(1)} %get-tuple-element.53), channel_id=1, source_target_pairs={{0,4},{1,5},{2,6},{3,7},{4,0},{5,1},{6,2},{7,3},{8,12},{9,13},{10,... | collective-permute-start | bytes 1769480 | tf_op jit(solution)/shard_map/ppermute | solution.py:10
  181.6 41.1 %collective-permute-start.11 = (f32[384,384]{1,0:T(8,128)S(1)}, f32[384,384]{1,0:T(8,128)}, u32[]{:S(2)}, u32[]{:S(2)}) collective-permute-start(f32[384,384]{1,0:T(8,128)S(1)} %get-tuple-element.49), channel_id=1, source_target_pairs={{0,4},{1,5},{2,6},{3,7},{4,0},{5,1},{6,2},{7,3},{8,12},{9,13},{10,... | collective-permute-start | bytes 1769480 | tf_op jit(solution)/shard_map/ppermute | solution.py:10
  183.7 39.1 %collective-permute-start.12 = (f32[384,384]{1,0:T(8,128)S(1)}, f32[384,384]{1,0:T(8,128)}, u32[]{:S(2)}, u32[]{:S(2)}) collective-permute-start(f32[384,384]{1,0:T(8,128)S(1)} %get-tuple-element.50), channel_id=1, source_target_pairs={{0,4},{1,5},{2,6},{3,7},{4,0},{5,1},{6,2},{7,3},{8,12},{9,13},{10,... | collective-permute-start | bytes 1769480 | tf_op jit(solution)/shard_map/ppermute | solution.py:10
  183.7 37.9 %collective-permute-start.13 = (f32[1,384]{1,0:T(1,128)S(1)}, f32[1,384]{1,0:T(1,128)S(1)}, u32[]{:S(2)}, u32[]{:S(2)}) collective-permute-start(f32[1,384]{1,0:T(1,128)S(1)} %get-tuple-element.51), channel_id=1, source_target_pairs={{0,4},{1,5},{2,6},{3,7},{4,0},{5,1},{6,2},{7,3},{8,12},{9,13},{10,... | collective-permute-start | bytes 4616 | tf_op jit(solution)/shard_map/ppermute | solution.py:10
  185.7 35.9 %collective-permute-start.14 = (f32[1,384]{1,0:T(1,128)S(1)}, f32[1,384]{1,0:T(1,128)S(1)}, u32[]{:S(2)}, u32[]{:S(2)}) collective-permute-start(f32[1,384]{1,0:T(1,128)S(1)} %get-tuple-element.52), channel_id=1, source_target_pairs={{0,4},{1,5},{2,6},{3,7},{4,0},{5,1},{6,2},{7,3},{8,12},{9,13},{10,... | collective-permute-start | bytes 4616 | tf_op jit(solution)/shard_map/ppermute | solution.py:10
  246.6 27.5 %collective-permute-start.16 = (f32[384,384]{1,0:T(8,128)S(1)}, f32[384,384]{1,0:T(8,128)}, u32[]{:S(2)}, u32[]{:S(2)}) collective-permute-start(f32[384,384]{1,0:T(8,128)S(1)} %broadcast_select_fusion), channel_id=1, source_target_pairs={{0,8},{1,9},{2,10},{3,11},{4,12},{5,13},{6,14},{7,15},{8,0},{9,1},... | collective-permute-start | bytes 1769480 | tf_op jit(solution)/shard_map/ppermute | solution.py:10
  246.7 27.4 %collective-permute-start.17 = (f32[1,384]{1,0:T(1,128)S(1)}, f32[1,384]{1,0:T(1,128)S(1)}, u32[]{:S(2)}, u32[]{:S(2)}) collective-permute-start(f32[1,384]{1,0:T(1,128)S(1)} %broadcast_select_fusion.13), channel_id=1, source_target_pairs={{0,8},{1,9},{2,10},{3,11},{4,12},{5,13},{6,14},{7,15},{8,0},{9,1},... | collective-permute-start | bytes 4616 | tf_op jit(solution)/shard_map/ppermute | solution.py:10
  274.1 16.6 %copy-start.12 = (f32[384,384]{1,0:T(8,128)S(1)}, f32[384,384]{1,0:T(8,128)}, u32[]{:S(2)}) copy-start(f32[384,384]{1,0:T(8,128)} %copy-done.11) | copy-start | bytes 1769476
  275.3 15.8 %copy-start.10 = (f32[384,384]{1,0:T(8,128)S(1)}, f32[384,384]{1,0:T(8,128)}, u32[]{:S(2)}) copy-start(f32[384,384]{1,0:T(8,128)} %copy-done.9) | copy-start | bytes 1769476
  275.3 16.5 %copy-start.8 = (f32[384,384]{1,0:T(8,128)S(1)}, f32[384,384]{1,0:T(8,128)}, u32[]{:S(2)}) copy-start(f32[384,384]{1,0:T(8,128)} %copy-done.7) | copy-start | bytes 1769476
  289.9 3.0 copy-start.4
  (12 other events, 18.8 us)
Sparse Core Ops, SparseCore 0:
  9.6 42.3 all-gather.1
